TPU v7x, 32 devices: a whole 2x2x4 slice. The times are simulated.
32 devices in a mesh: prow: 8 (over y, x, core), pcol: 4 (over z).
Axes of the slice: x: 2, y: 2, z: 4, core: 2. Of those that a mesh axis runs over, the one named last changes fastest.
Arguments:
- inverse: bfloat16 [4, 4096, 8, 2048], P(None, 'prow', None, 'pcol'), may hold values from -6 to 6
- panel: bfloat16 [2, 4, 4096, 256], P(None, None, 'prow'), may hold values from -0.09375 to 0.09375
- structure: int32 [2, 8], replicated, may hold values from 0 to 31, as said below
- diag_inverse: float32 [2, 256, 256], replicated, may hold values from -6 to 6
Outputs:
- off_diag: bfloat16 [2, 4, 4096, 256], P(None, None, ('prow', 'pcol'))
- diag_block: float32 [2, 256, 256], replicated
Inputs may be any that keep to these rules, and one draw needn't show every extreme that they name: `structure`: each row lists 8 distinct block indices in increasing order, exactly one of them congruent to p modulo 8 for every p, and always includes the last ancestor block 31.
All inputs are finite; a program needn't handle non-finite values.
Results may differ from a plain program's by a relative error of at most 0.0022.
Values may be sent and summed in bfloat16 or wider, within the bound.
A program may use at most 128 MiB of HBM per device.

v0:
```python
import functools

import jax
import jax.numpy as jnp
from jax import lax
from jax.experimental import pallas as pl
from jax.experimental.pallas import tpu as pltpu
from jax.sharding import PartitionSpec as P

MESH = pl.DeviceIdType.MESH
SUB = 2
STRIPS = 4


def remote(src, dst, send, recv, p, q):
    return pltpu.make_async_remote_copy(
        src_ref=src, dst_ref=dst, send_sem=send, recv_sem=recv, device_id=(p, q), device_id_type=MESH
    )


def fused(
    n_rows, n_cols, a_ref, l_ref, d_ref, y_ref, g_ref,
    l_buf, part, right_buf, left_buf, right_scale, left_scale, term, plane_buf, col_buf, gath,
    l_send, l_recv, r_send, r_recv, f_send, f_recv, p_send, p_recv, c_send, c_recv, g_send, g_recv,
):
    p = lax.axis_index("prow")
    q = lax.axis_index("pcol")
    nodes, ratio, block, width = l_buf.shape
    piece = block // n_cols
    seg = width // n_rows
    chunk = block // (2 * SUB)
    hi = p // n_cols
    lo = p % n_cols
    t = jnp.int32(0)
    bit = 1
    while bit < n_cols:
        t = t + bit * (((lo // bit) + (q // bit)) % 2)
        bit *= 2
    pair = p + 1 - 2 * (p % 2)

    def beside(j):
        lo2 = jnp.int32(0)
        b = 1
        while b < n_cols:
            lo2 = lo2 + b * (((lo // b) + (2 * j // b)) % 2)
            b *= 2
        return hi * n_cols + lo2

    barrier = pltpu.get_barrier_semaphore()
    for k in range(1, n_rows):
        pl.semaphore_signal(barrier, inc=1, device_id=((p + k) % n_rows, q), device_id_type=MESH)
    for k in range(1, n_cols):
        pl.semaphore_signal(barrier, inc=1, device_id=(p, (q + k) % n_cols), device_id_type=MESH)
    pl.semaphore_wait(barrier, n_rows + n_cols - 2)

    def rows(c):
        return pl.ds(pl.multiple_of(c * chunk, chunk), chunk)

    def l_slot(s, h, c):
        return l_buf.at[s, h, rows(c)]

    def to_peer_hi(s, c, k, src):
        return remote(src, l_slot(s, hi, c), l_send.at[s, c, k - 1], l_recv.at[s, hi, c],
                      (p + k * n_cols) % n_rows, q)

    def to_x(s, c, j, src):
        return remote(src, l_slot(s, hi, c), l_send.at[s, c, ratio - 1 + j - 1], l_recv.at[s, hi, c],
                      beside(j), q)

    def to_pair(s, c, k, src):
        h = (hi + k) % ratio
        return remote(src, l_slot(s, h, c), l_send.at[s, c, ratio - 1 + n_cols // 2 - 1 + k],
                      l_recv.at[s, h, c], pair, q)

    def l_arrived(s, c, h):
        remote(l_slot(s, h, c), l_slot(s, h, c), l_send.at[s, c, 0], l_recv.at[s, h, c], pair, q).wait_recv()

    owner = t == 0
    source_chip = t < 2
    core = p % 2

    def mine(u):
        return core * SUB + u

    def other(u):
        return (1 - core) * SUB + u

    @pl.when(owner)
    def _():
        for s in range(nodes):
            for u in range(SUB):
                to_pair(s, other(u), 0, l_ref.at[s, rows(other(u))]).start()
            for u in range(SUB):
                src = l_ref.at[s, rows(mine(u))]
                for j in range(1, n_cols // 2):
                    to_x(s, mine(u), j, src).start()
                for k in range(1, ratio):
                    to_peer_hi(s, mine(u), k, src).start()
            for u in range(SUB):
                to_pair(s, mine(u), 0, l_ref.at[s, rows(mine(u))]).start()
        for s in range(nodes):
            l_buf[s, hi] = l_ref[s]

    def receive_blocks(s):
        for u in range(SUB):
            c = mine(u)
            src = l_slot(s, hi, c)

            @pl.when(jnp.logical_not(owner))
            def _():
                l_arrived(s, c, hi)
                for k in range(1, ratio):
                    to_peer_hi(s, c, k, src).start()

            @pl.when(t == 1)
            def _():
                for j in range(1, n_cols // 2):
                    to_x(s, c, j, src).start()

            @pl.when(jnp.logical_not(source_chip))
            def _():
                to_pair(s, c, 0, src).start()

        for u in range(SUB):
            c = mine(u)
            for k in range(1, ratio):
                l_arrived(s, c, (hi + k) % ratio)
                to_pair(s, c, k, l_slot(s, (hi + k) % ratio, c)).start()
        for u in range(SUB):
            c = other(u)

            @pl.when(jnp.logical_not(owner))
            def _():
                l_arrived(s, c, hi)

            for k in range(1, ratio):
                l_arrived(s, c, (hi + k) % ratio)

    def drain_blocks(s):
        for u in range(SUB):
            c = mine(u)
            src = l_slot(s, hi, c)
            for k in range(1, ratio):
                to_peer_hi(s, c, k, src).wait_send()
                to_pair(s, c, k, src).wait_send()

            @pl.when(source_chip)
            def _():
                for j in range(1, n_cols // 2):
                    to_x(s, c, j, src).wait_send()

            @pl.when(t != 1)
            def _():
                to_pair(s, c, 0, src).wait_send()

            @pl.when(owner)
            def _():
                to_pair(s, other(u), 0, src).wait_send()

    def multiply(s):
        total = jnp.dot(a_ref[s, 0], l_buf[s, 0], preferred_element_type=jnp.float32)
        for h in range(1, ratio):
            total += jnp.dot(a_ref[s, h], l_buf[s, h], preferred_element_type=jnp.float32)
        for d in range(n_cols):
            part[s, d] = total[d * piece:(d + 1) * piece]
        return total

    def diagonal_term(s, total):
        high = total.astype(jnp.bfloat16)
        low = (total - high.astype(jnp.float32)).astype(jnp.bfloat16)
        over_rows = (((0,), (0,)), ((), ()))
        product = lax.dot_general(l_ref[s], high, over_rows, preferred_element_type=jnp.float32)
        product += lax.dot_general(l_ref[s], low, over_rows, preferred_element_type=jnp.float32)
        for k in range(n_rows):
            term[s, k] = product[k * seg:(k + 1) * seg]

    def encode(s, d, value, buf, scale):
        largest = jnp.maximum(jnp.max(jnp.abs(value), axis=0, keepdims=True), 1e-30)
        buf[s, d] = jnp.floor(value * (32700.0 / largest) + 0.5).astype(jnp.int32).astype(jnp.int16)
        scale[s, d] = jnp.broadcast_to(largest * (1.0 / 32700.0), scale.shape[2:])

    def decode(s, d, buf, scale):
        return buf[s, d].astype(jnp.int32).astype(jnp.float32) * scale[s, d][0:1]

    class line_copy:
        def __init__(self, s, d, buf, scale, send, recv, to):
            self.copies = [
                remote(buf.at[s, d], buf.at[s, d], send.at[0, s, d], recv.at[0, s, d], p, to),
                remote(scale.at[s, d], scale.at[s, d], send.at[1, s, d], recv.at[1, s, d], p, to),
            ]

        def start(self):
            for copy in self.copies:
                copy.start()

        def wait_send(self):
            for copy in self.copies:
                copy.wait_send()

        def wait_recv(self):
            for copy in self.copies:
                copy.wait_recv()

    def right_copy(s, d):
        return line_copy(s, d, right_buf, right_scale, r_send, r_recv, (q + 1) % n_cols)

    def left_copy(s, d):
        return line_copy(s, d, left_buf, left_scale, f_send, f_recv, (q + n_cols - 1) % n_cols)

    def line_start(s, nearest):
        @pl.when(q == 0)
        def _():
            for d in ((1,) if nearest else range(n_cols - 1, 1, -1)):
                encode(s, d, part[s, d], right_buf, right_scale)
                right_copy(s, d).start()

        @pl.when(q == n_cols - 1)
        def _():
            for d in ((n_cols - 2,) if nearest else range(n_cols - 2)):
                encode(s, d, part[s, d], left_buf, left_scale)
                left_copy(s, d).start()

    def line_relay(s):
        for i in range(n_cols - 2):
            d = n_cols - 1 - i

            @pl.when(jnp.logical_and(q > 0, q < d))
            def _():
                right_copy(s, d).wait_recv()
                encode(s, d, decode(s, d, right_buf, right_scale) + part[s, d], right_buf, right_scale)
                right_copy(s, d).start()

            e = i

            @pl.when(jnp.logical_and(q < n_cols - 1, q > e))
            def _():
                left_copy(s, e).wait_recv()
                encode(s, e, decode(s, e, left_buf, left_scale) + part[s, e], left_buf, left_scale)
                left_copy(s, e).start()

    def line_finish(s):
        @pl.when(q > 0)
        def _():
            right_copy(s, q).wait_recv()
            part[s, q] = part[s, q] + decode(s, q, right_buf, right_scale)

        @pl.when(q < n_cols - 1)
        def _():
            left_copy(s, q).wait_recv()
            part[s, q] = part[s, q] + decode(s, q, left_buf, left_scale)

        y_ref[s] = (-part[s, q]).astype(jnp.bfloat16)

    def line_drain(s):
        for d in range(n_cols):
            @pl.when(q < d)
            def _():
                right_copy(s, d).wait_send()

            @pl.when(q > d)
            def _():
                left_copy(s, d).wait_send()

    def plane_copy(s, k):
        to = (p + k) % n_rows
        return remote(term.at[s, to], plane_buf.at[s, n_rows - k], p_send.at[s, k], p_recv.at[s, n_rows - k], to, q)

    def plane_wait(s, k):
        remote(term.at[s, 0], plane_buf.at[s, k], p_send.at[s, k], p_recv.at[s, k], pair, q).wait_recv()

    def col_copy(s, k):
        to = (q + k) % n_cols
        return remote(col_buf.at[s, q], col_buf.at[s, q], c_send.at[s, k], c_recv.at[s, n_cols - k], p, to)

    def col_wait(s, k):
        src = (q + k) % n_cols
        remote(col_buf.at[s, src], col_buf.at[s, src], c_send.at[s, k], c_recv.at[s, k], pair, q).wait_recv()

    def gath_copy(s, k):
        to = (p + k) % n_rows
        return remote(gath.at[s, p], gath.at[s, p], g_send.at[s, k], g_recv.at[s, n_rows - k], to, q)

    def gath_wait(s, k):
        src = (p + k) % n_rows
        remote(gath.at[s, src], gath.at[s, src], g_send.at[s, k], g_recv.at[s, k], pair, q).wait_recv()

    def plane_start(s):
        for k in range(1, n_rows):
            plane_copy(s, k).start()

    def col_start(s):
        total = term[s, p]
        for k in range(1, n_rows):
            plane_wait(s, k)
            total = total + plane_buf[s, k]
        col_buf[s, q] = total
        for k in range(1, n_cols):
            col_copy(s, k).start()

    def gath_start(s):
        for k in range(1, n_cols):
            col_wait(s, k)
        total = col_buf[s, 0]
        for k in range(1, n_cols):
            total = total + col_buf[s, k]
        gath[s, p] = d_ref[s, pl.ds(pl.multiple_of(p * seg, seg), seg)] + total
        for k in range(1, n_rows):
            gath_copy(s, k).start()

    for s in range(nodes):
        receive_blocks(s)
        total = multiply(s)
        if s > 0:
            col_start(s - 1)
            line_start(s - 1, True)
        line_start(s, False)
        diagonal_term(s, total)
        plane_start(s)
    for s in range(nodes):
        line_relay(s)
        if s == 0:
            col_start(nodes - 1)
            line_start(nodes - 1, True)
        if s < nodes - 1:
            gath_start(s)
    gath_start(nodes - 1)
    for s in range(nodes):
        line_finish(s)
    for s in range(nodes):
        drain_blocks(s)
        line_drain(s)
        for k in range(1, n_rows):
            plane_copy(s, k).wait_send()
        for k in range(1, n_cols):
            col_copy(s, k).wait_send()
    for s in range(nodes):
        for k in range(1, n_rows):
            gath_wait(s, k)
        for k in range(n_rows):
            g_ref[s, k * seg:(k + 1) * seg] = gath[s, k]
    for s in range(nodes):
        for k in range(1, n_rows):
            gath_copy(s, k).wait_send()


def pick(
    n_rows, n_cols, structure_ref, inverse_ref, panel_ref, a_ref, l_ref, mask_ref, raw, wide, a_sem, l_sem
):
    p = lax.axis_index("prow")
    q = lax.axis_index("pcol")
    nodes, ratio, block, _ = a_ref.shape
    _, strips, strip, cols_local, _ = raw.shape
    rows_local = inverse_ref.shape[0]
    listed = structure_ref.shape[1]

    def find(s, residue, divisor):
        found = jnp.int32(0)
        for i in range(listed):
            value = structure_ref[s, i]
            found = found + jnp.where(value % n_rows == residue, value // divisor, 0)
        return found

    copies = []
    for s in range(nodes):
        row = find(s, p, n_rows)
        factor = pltpu.make_async_copy(panel_ref.at[s, row], l_ref.at[s], l_sem.at[s])
        factor.start()
        copies.append(factor)
        for k in range(strips):
            pltpu.make_async_copy(
                inverse_ref.at[row, pl.ds(k * strip, strip)], raw.at[s, k], a_sem.at[s, k]
            ).start()
        for r in range(rows_local):
            mask_ref[s, r] = jnp.where(row == r, 1, 0).astype(jnp.int32)
    for s in range(nodes):
        cols = [find(s, h * n_cols + q, n_cols) for h in range(ratio)]
        for k in range(strips):
            pltpu.make_async_copy(
                inverse_ref.at[0, pl.ds(k * strip, strip)], raw.at[s, k], a_sem.at[s, k]
            ).wait()
            slot = k % 2
            for b in range(block // 128):
                lanes = raw[s, k, :, :, b * 128:(b + 1) * 128].astype(jnp.float32)
                wide[slot, b] = lanes.reshape(strip * cols_local, 128)
            for h in range(ratio):
                for b in range(block // 128):
                    a_ref[s, h, k * strip:(k + 1) * strip, b * 128:(b + 1) * 128] = wide[
                        slot, b, pl.ds(cols[h], strip, stride=cols_local)
                    ].astype(jnp.bfloat16)
    for factor in copies:
        factor.wait()


def on_device(inverse, panel, structure, diag_inverse):
    n_rows = lax.axis_size("prow")
    n_cols = lax.axis_size("pcol")
    rows_local, block, cols_local, _ = inverse.shape
    nodes, _, _, width = panel.shape
    ratio = n_rows // n_cols
    piece = block // n_cols
    seg = width // n_rows
    strip = block // STRIPS

    vmem = pl.BlockSpec(memory_space=pltpu.VMEM)
    smem = pl.BlockSpec(memory_space=pltpu.SMEM)
    hbm = pl.BlockSpec(memory_space=pltpu.HBM)
    a_sel, l_sel, mask = pl.pallas_call(
        functools.partial(pick, n_rows, n_cols),
        out_shape=(
            jax.ShapeDtypeStruct((nodes, ratio, block, block), jnp.bfloat16),
            jax.ShapeDtypeStruct((nodes, block, width), jnp.bfloat16),
            jax.ShapeDtypeStruct((nodes, rows_local), jnp.int32),
        ),
        in_specs=[smem, hbm, hbm],
        out_specs=(vmem, vmem, smem),
        scratch_shapes=[
            pltpu.VMEM((nodes, STRIPS, strip, cols_local, block), jnp.bfloat16),
            pltpu.VMEM((2, block // 128, strip * cols_local, 128), jnp.float32),
            pltpu.SemaphoreType.DMA((nodes, STRIPS)),
            pltpu.SemaphoreType.DMA((nodes,)),
        ],
        compiler_params=pltpu.CompilerParams(vmem_limit_bytes=50 * 1024 * 1024),
        name="pick_blocks",
    )(structure, inverse, panel)

    f32 = jnp.float32
    dma = pltpu.SemaphoreType.DMA
    sends = ratio - 1 + n_cols // 2 - 1 + ratio
    pieces, diagonal = pl.pallas_call(
        functools.partial(fused, n_rows, n_cols),
        out_shape=(
            jax.ShapeDtypeStruct((nodes, piece, width), jnp.bfloat16),
            jax.ShapeDtypeStruct((nodes, width, width), f32),
        ),
        in_specs=[vmem] * 3,
        out_specs=(vmem, vmem),
        scratch_shapes=[
            pltpu.VMEM((nodes, ratio, block, width), jnp.bfloat16),
            pltpu.VMEM((nodes, n_cols, piece, width), f32),
            pltpu.VMEM((nodes, n_cols, piece, width), jnp.int16),
            pltpu.VMEM((nodes, n_cols, piece, width), jnp.int16),
            pltpu.VMEM((nodes, n_cols, 8, width), f32),
            pltpu.VMEM((nodes, n_cols, 8, width), f32),
            pltpu.VMEM((nodes, n_rows, seg, width), f32),
            pltpu.VMEM((nodes, n_rows, seg, width), f32),
            pltpu.VMEM((nodes, n_cols, seg, width), f32),
            pltpu.VMEM((nodes, n_rows, seg, width), f32),
            dma((nodes, 2 * SUB, sends)), dma((nodes, ratio, 2 * SUB)),
            dma((2, nodes, n_cols)), dma((2, nodes, n_cols)),
            dma((2, nodes, n_cols)), dma((2, nodes, n_cols)),
            dma((nodes, n_rows)), dma((nodes, n_rows)),
            dma((nodes, n_cols)), dma((nodes, n_cols)),
            dma((nodes, n_rows)), dma((nodes, n_rows)),
        ],
        compiler_params=pltpu.CompilerParams(
            collective_id=0, has_side_effects=True, vmem_limit_bytes=40 * 1024 * 1024
        ),
        name="selected_inverse",
    )(a_sel, l_sel, diag_inverse)

    off_diag = jnp.where(mask[:, :, None, None] > 0, pieces[:, None], jnp.zeros((), jnp.bfloat16))
    return off_diag, diagonal


def solution(mesh):
    placed = (P(None, "prow", None, "pcol"), P(None, None, "prow", None), P(), P())
    return jax.shard_map(
        on_device,
        mesh=mesh,
        in_specs=placed,
        out_specs=(P(None, None, ("prow", "pcol"), None), P()),
        check_vma=False,
    )
```

profile of v0, /device:TPU:9, one launch (start us, length us, event | category | flops | bytes accessed | tf_op | source)
XLA Modules:
  0.0 56.0 jit_solution(8295043415837479433)
XLA Ops:
  0.6 0.0 copy-start
  0.6 0.0 copy-start.1
  0.7 0.7 %copy-done.1 = s32[2,8]{1,0:T(2,128)S(1)} copy-done((s32[2,8]{1,0:T(2,128)S(1)}, s32[2,8]{1,0:T(2,128)}, u32[]{:S(2)}) %copy-start.1) | copy-done | bytes 88
  1.4 5.2 %pick_blocks.1 = (bf16[2,2,512,512]{3,2,1,0:T(8,128)(2,1)S(1)}, bf16[2,512,256]{2,1,0:T(8,128)(2,1)S(1)}, s32[2,4]{1,0:T(2,128)S(1)}) custom-call(s32[2,8]{1,0:T(2,128)S(1)} %copy-done.1, bf16[4,512,8,512]{3,2,1,0:T(8,128)(2,1)} %inverse_ref.1, bf16[2,4,512,256]{3,2,1,0:T(8,128)(2,1)} %panel_ref.1), custom_call_target="tpu_custom_call" | custom-call | tf_op jit(solution)/shard_map/pick_blocks/pallas_call | solution.py:407
  6.5 0.0 copy-done
  6.6 47.7 %selected_inverse.1 = (bf16[2,128,256]{2,1,0:T(8,128)(2,1)S(1)}, f32[2,256,256]{2,1,0:T(8,128)S(1)}) custom-call(bf16[2,2,512,512]{3,2,1,0:T(8,128)(2,1)S(1)} %get-tuple-element.8.a_ref, bf16[2,512,256]{2,1,0:T(8,128)(2,1)S(1)} %get-tuple-element.9.l_ref, f32[2,256,256]{2,1,0:T(8,128)S(1)} %copy-done), custom_call_target="tpu_custom_call" | custom-call | tf_op jit(solution)/shard_map/selected_inverse/pallas_call | solution.py:429
  54.3 0.9 %broadcast_select_fusion = bf16[2,4,128,256]{3,2,1,0:T(8,128)(2,1)} fusion(pred[2,4]{1,0:T(4,128)(4,1)S(1)} %broadcast_compare_fusion, bf16[2,128,256]{2,1,0:T(8,128)(2,1)S(1)} %get-tuple-element.10), kind=kLoop, calls=%fused_computation | loop fusion | flops 262144 | bytes 655368 | tf_op jit(solution)/shard_map/jit(_where)/select_n | solution.py:461
  55.2 0.8 %copy.7 = f32[2,256,256]{2,1,0:T(8,128)} copy(f32[2,256,256]{2,1,0:T(8,128)S(1)} %get-tuple-element.15) | data formatting | bytes 1048576
  (1 shorter events, 0.0 us)
Async XLA Ops:
  0.6 5.9 %copy-start = (f32[2,256,256]{2,1,0:T(8,128)S(1)}, f32[2,256,256]{2,1,0:T(8,128)}, u32[]{:S(2)}) copy-start(f32[2,256,256]{2,1,0:T(8,128)} %d_ref.1) | copy-start | bytes 1572868
  0.6 0.7 %copy-start.1 = (s32[2,8]{1,0:T(2,128)S(1)}, s32[2,8]{1,0:T(2,128)}, u32[]{:S(2)}) copy-start(s32[2,8]{1,0:T(2,128)} %structure_ref.1) | copy-start | bytes 196
where the time goes:
time: 57 us; the launch traced here: 56 us
  Pallas kernels  52.9 us (93%)
  local copies, waits for them, and re-layouts  1.53 us (3%)
  other arithmetic  0.91 us (2%)
  between operations  0.68 us (1%)
    pallas_call x1, Pallas kernels, on_device(): pl.pallas_call(functools.partial(fused, n_rows, n_cols), out_shape=(jax.S...  47.7 us
    pallas_call x1, Pallas kernels, on_device(): pl.pallas_call(functools.partial(pick, n_rows, n_cols), out_shape=(jax.Sh...  5.15 us
    unnamed x5, local copies, waits for them, and re-layouts  1.53 us

commit v1 on v0

v1 whole, which is shorter than its diff:
```python
import functools

import jax
import jax.numpy as jnp
from jax import lax
from jax.experimental import pallas as pl
from jax.experimental.pallas import tpu as pltpu
from jax.sharding import PartitionSpec as P

MESH = pl.DeviceIdType.MESH
SUB = 2
STRIPS = 8
FULL = 32700.0


def remote(src, dst, send, recv, p, q):
    return pltpu.make_async_remote_copy(
        src_ref=src, dst_ref=dst, send_sem=send, recv_sem=recv, device_id=(p, q), device_id_type=MESH
    )


def scope(name):
    return jax.named_scope(name)


def selected(
    n_rows, n_cols, structure_hbm, inverse_ref, panel_ref, d_ref, y_ref, g_ref,
    structure_ref, panel_buf, raw, wide, a_ref, l_ref, l_buf, part,
    right_buf, left_buf, right_scale, left_scale,
    term, term_buf, term_scale, plane_buf, plane_scale, col_buf, col_scale, gath, gath_scale,
    s_sem, n_sem, a_sem,
    l_send, l_recv, r_send, r_recv, f_send, f_recv, p_send, p_recv, c_send, c_recv, g_send, g_recv,
):
    p = lax.axis_index("prow")
    q = lax.axis_index("pcol")
    nodes, ratio, block, width = l_buf.shape
    rows_local, _, cols_local, _ = inverse_ref.shape
    listed = structure_ref.shape[1]
    piece = block // n_cols
    seg = width // n_rows
    chunk = block // (2 * SUB)
    strip = block // STRIPS
    hi = p // n_cols
    lo = p % n_cols
    t = jnp.int32(0)
    bit = 1
    while bit < n_cols:
        t = t + bit * (((lo // bit) + (q // bit)) % 2)
        bit *= 2
    pair = p + 1 - 2 * (p % 2)

    def beside(j):
        lo2 = jnp.int32(0)
        b = 1
        while b < n_cols:
            lo2 = lo2 + b * (((lo // b) + (2 * j // b)) % 2)
            b *= 2
        return hi * n_cols + lo2

    structure_copy = pltpu.make_async_copy(structure_hbm, structure_ref, s_sem)
    structure_copy.start()
    panel_copies = [pltpu.make_async_copy(panel_ref.at[s], panel_buf[s], n_sem.at[s]) for s in range(nodes)]
    for copy in panel_copies:
        copy.start()

    def strip_copy(k):
        part_of = pl.ds(k * strip, strip)
        return pltpu.make_async_copy(inverse_ref.at[:, part_of], raw[k], a_sem.at[k])

    for k in range(STRIPS):
        strip_copy(k).start()

    barrier = pltpu.get_barrier_semaphore()
    for k in range(1, n_rows):
        pl.semaphore_signal(barrier, inc=1, device_id=((p + k) % n_rows, q), device_id_type=MESH)
    for k in range(1, n_cols):
        pl.semaphore_signal(barrier, inc=1, device_id=(p, (q + k) % n_cols), device_id_type=MESH)

    def find(s, residue, divisor):
        found = jnp.int32(0)
        for i in range(listed):
            value = structure_ref[s, i]
            found = found + jnp.where(value % n_rows == residue, value // divisor, 0)
        return found

    with scope("pickl"):
        structure_copy.wait()
        row = [find(s, p, n_rows) for s in range(nodes)]
        cols = [[find(s, h * n_cols + q, n_cols) for h in range(ratio)] for s in range(nodes)]
        for s in range(nodes):
            panel_copies[s].wait()
            l_ref[s] = panel_buf[s][row[s]]

    with scope("barrier"):
        pl.semaphore_wait(barrier, n_rows + n_cols - 2)

    def rows(c):
        return pl.ds(pl.multiple_of(c * chunk, chunk), chunk)

    def l_slot(s, h, c):
        return l_buf.at[s, h, rows(c)]

    def to_peer_hi(s, c, k, src):
        return remote(src, l_slot(s, hi, c), l_send.at[s, c, k - 1], l_recv.at[s, hi, c],
                      (p + k * n_cols) % n_rows, q)

    def to_x(s, c, j, src):
        return remote(src, l_slot(s, hi, c), l_send.at[s, c, ratio - 1 + j - 1], l_recv.at[s, hi, c],
                      beside(j), q)

    def to_pair(s, c, k, src):
        h = (hi + k) % ratio
        return remote(src, l_slot(s, h, c), l_send.at[s, c, ratio - 1 + n_cols // 2 - 1 + k],
                      l_recv.at[s, h, c], pair, q)

    def l_arrived(s, c, h):
        remote(l_slot(s, h, c), l_slot(s, h, c), l_send.at[s, c, 0], l_recv.at[s, h, c], pair, q).wait_recv()

    owner = t == 0
    source_chip = t < 2
    core = p % 2

    def mine(u):
        return core * SUB + u

    def other(u):
        return (1 - core) * SUB + u

    @pl.when(owner)
    def _():
        for s in range(nodes):
            for u in range(SUB):
                to_pair(s, other(u), 0, l_ref.at[s, rows(other(u))]).start()
            for u in range(SUB):
                src = l_ref.at[s, rows(mine(u))]
                for j in range(1, n_cols // 2):
                    to_x(s, mine(u), j, src).start()
                for k in range(1, ratio):
                    to_peer_hi(s, mine(u), k, src).start()
            for u in range(SUB):
                to_pair(s, mine(u), 0, l_ref.at[s, rows(mine(u))]).start()
        for s in range(nodes):
            l_buf[s, hi] = l_ref[s]

    def own_from_pair(s, u):
        c = mine(u)

        @pl.when(t == 1)
        def _():
            l_arrived(s, c, hi)
            for j in range(1, n_cols // 2):
                to_x(s, c, j, l_slot(s, hi, c)).start()
            for k in range(1, ratio):
                to_peer_hi(s, c, k, l_slot(s, hi, c)).start()

    def own_from_x(s, u):
        c = mine(u)

        @pl.when(jnp.logical_not(source_chip))
        def _():
            l_arrived(s, c, hi)
            for k in range(1, ratio):
                to_peer_hi(s, c, k, l_slot(s, hi, c)).start()
            to_pair(s, c, 0, l_slot(s, hi, c)).start()

    def others_from_hi(s, u):
        c = mine(u)
        for k in range(1, ratio):
            l_arrived(s, c, (hi + k) % ratio)
            to_pair(s, c, k, l_slot(s, (hi + k) % ratio, c)).start()

    def rest(s):
        for u in range(SUB):
            c = other(u)

            @pl.when(jnp.logical_not(owner))
            def _():
                l_arrived(s, c, hi)

            for k in range(1, ratio):
                l_arrived(s, c, (hi + k) % ratio)

    def drain_blocks(s):
        for u in range(SUB):
            c = mine(u)
            src = l_slot(s, hi, c)
            for k in range(1, ratio):
                to_peer_hi(s, c, k, src).wait_send()
                to_pair(s, c, k, src).wait_send()

            @pl.when(source_chip)
            def _():
                for j in range(1, n_cols // 2):
                    to_x(s, c, j, src).wait_send()

            @pl.when(t != 1)
            def _():
                to_pair(s, c, 0, src).wait_send()

            @pl.when(owner)
            def _():
                to_pair(s, other(u), 0, src).wait_send()

    def choose(k):
        strip_copy(k).wait()
        for s in range(nodes):
            for b in range(block // 128):
                lanes = raw[k][row[s], :, :, b * 128:(b + 1) * 128].astype(jnp.float32)
                wide[s, b] = lanes.reshape(strip * cols_local, 128)
            for h in range(ratio):
                for b in range(block // 128):
                    a_ref[s, h, k * strip:(k + 1) * strip, b * 128:(b + 1) * 128] = wide[
                        s, b, pl.ds(cols[s][h], strip, stride=cols_local)
                    ].astype(jnp.bfloat16)

    def multiply(s):
        total = jnp.dot(a_ref[s, 0], l_buf[s, 0], preferred_element_type=jnp.float32)
        for h in range(1, ratio):
            total += jnp.dot(a_ref[s, h], l_buf[s, h], preferred_element_type=jnp.float32)
        for d in range(n_cols):
            part[s, d] = total[d * piece:(d + 1) * piece]
        return total

    def encoded(value):
        largest = jnp.maximum(jnp.max(jnp.abs(value), axis=0, keepdims=True), 1e-30)
        whole = jnp.floor(value * (FULL / largest) + 0.5).astype(jnp.int32).astype(jnp.int16)
        return whole, largest * (1.0 / FULL)

    def decoded(whole, scale):
        return whole.astype(jnp.int32).astype(jnp.float32) * scale

    def diagonal_term(s, total):
        high = total.astype(jnp.bfloat16)
        low = (total - high.astype(jnp.float32)).astype(jnp.bfloat16)
        over_rows = (((0,), (0,)), ((), ()))
        product = lax.dot_general(l_ref[s], high, over_rows, preferred_element_type=jnp.float32)
        product += lax.dot_general(l_ref[s], low, over_rows, preferred_element_type=jnp.float32)
        whole, scale = encoded(product)
        term_scale[s] = scale
        for k in range(n_rows):
            term[s, k] = product[k * seg:(k + 1) * seg]
            term_buf[s, k] = whole[k * seg:(k + 1) * seg]

    class both:
        def __init__(self, src, src_scale, dst, dst_scale, send, recv, send_at, recv_at, to_p, to_q):
            self.copies = [
                remote(src, dst, send.at[(0, *send_at)], recv.at[(0, *recv_at)], to_p, to_q),
                remote(src_scale, dst_scale, send.at[(1, *send_at)], recv.at[(1, *recv_at)], to_p, to_q),
            ]

        def start(self):
            for copy in self.copies:
                copy.start()

        def wait_send(self):
            for copy in self.copies:
                copy.wait_send()

        def wait_recv(self):
            for copy in self.copies:
                copy.wait_recv()

    def right_copy(s, d):
        return both(right_buf.at[s, d], right_scale.at[s, d], right_buf.at[s, d], right_scale.at[s, d],
                    r_send, r_recv, (s, d), (s, d), p, (q + 1) % n_cols)

    def left_copy(s, d):
        return both(left_buf.at[s, d], left_scale.at[s, d], left_buf.at[s, d], left_scale.at[s, d],
                    f_send, f_recv, (s, d), (s, d), p, (q + n_cols - 1) % n_cols)

    def right_send(s, d, value):
        right_buf[s, d], right_scale[s, d] = encoded(value)
        right_copy(s, d).start()

    def left_send(s, d, value):
        left_buf[s, d], left_scale[s, d] = encoded(value)
        left_copy(s, d).start()

    def line_start(s, nearest):
        @pl.when(q == 0)
        def _():
            for d in ((1,) if nearest else range(n_cols - 1, 1, -1)):
                right_send(s, d, part[s, d])

        @pl.when(q == n_cols - 1)
        def _():
            for d in ((n_cols - 2,) if nearest else range(n_cols - 2)):
                left_send(s, d, part[s, d])

    def relay_right(s):
        for d in range(n_cols - 1, 1, -1):
            @pl.when(jnp.logical_and(q > 0, q < d))
            def _():
                right_copy(s, d).wait_recv()
                right_send(s, d, decoded(right_buf[s, d], right_scale[s, d]) + part[s, d])

    def relay_left(s):
        for e in range(n_cols - 2):
            @pl.when(jnp.logical_and(q < n_cols - 1, q > e))
            def _():
                left_copy(s, e).wait_recv()
                left_send(s, e, decoded(left_buf[s, e], left_scale[s, e]) + part[s, e])

    left_half = 2 * q < n_cols - 1

    def relay(s, first):
        @pl.when(left_half)
        def _():
            (relay_right if first else relay_left)(s)

        @pl.when(jnp.logical_not(left_half))
        def _():
            (relay_left if first else relay_right)(s)

    def line_finish(s):
        @pl.when(q > 0)
        def _():
            right_copy(s, q).wait_recv()
            part[s, q] = part[s, q] + decoded(right_buf[s, q], right_scale[s, q])

        @pl.when(q < n_cols - 1)
        def _():
            left_copy(s, q).wait_recv()
            part[s, q] = part[s, q] + decoded(left_buf[s, q], left_scale[s, q])

        value = (-part[s, q]).astype(jnp.bfloat16)
        for r in range(rows_local):
            y_ref[s, r] = jnp.where(row[s] == r, value, jnp.zeros_like(value))

    def line_drain(s):
        for d in range(n_cols):
            @pl.when(q < d)
            def _():
                right_copy(s, d).wait_send()

            @pl.when(q > d)
            def _():
                left_copy(s, d).wait_send()

    def plane_copy(s, k):
        to = (p + k) % n_rows
        return both(term_buf.at[s, to], term_scale.at[s], plane_buf.at[s, n_rows - k], plane_scale.at[s, n_rows - k],
                    p_send, p_recv, (s, k), (s, n_rows - k), to, q)

    def plane_wait(s, k):
        both(term_buf.at[s, 0], term_scale.at[s], plane_buf.at[s, k], plane_scale.at[s, k],
             p_send, p_recv, (s, k), (s, k), pair, q).wait_recv()

    def col_copy(s, k):
        to = (q + k) % n_cols
        return both(col_buf.at[s, q], col_scale.at[s, q], col_buf.at[s, q], col_scale.at[s, q],
                    c_send, c_recv, (s, k), (s, n_cols - k), p, to)

    def col_wait(s, k):
        src = (q + k) % n_cols
        both(col_buf.at[s, src], col_scale.at[s, src], col_buf.at[s, src], col_scale.at[s, src],
             c_send, c_recv, (s, k), (s, k), pair, q).wait_recv()

    def gath_copy(s, k):
        to = (p + k) % n_rows
        return both(gath.at[s, p], gath_scale.at[s, p], gath.at[s, p], gath_scale.at[s, p],
                    g_send, g_recv, (s, k), (s, n_rows - k), to, q)

    def gath_wait(s, k):
        src = (p + k) % n_rows
        both(gath.at[s, src], gath_scale.at[s, src], gath.at[s, src], gath_scale.at[s, src],
             g_send, g_recv, (s, k), (s, k), pair, q).wait_recv()

    def plane_start(s):
        for k in range(1, n_rows):
            plane_copy(s, k).start()

    def col_start(s):
        total = term[s, p]
        for k in range(1, n_rows):
            plane_wait(s, k)
            total = total + decoded(plane_buf[s, k], plane_scale[s, k])
        col_buf[s, q], col_scale[s, q] = encoded(total)
        for k in range(1, n_cols):
            col_copy(s, k).start()

    def gath_start(s):
        for k in range(1, n_cols):
            col_wait(s, k)
        total = decoded(col_buf[s, 0], col_scale[s, 0])
        for k in range(1, n_cols):
            total = total + decoded(col_buf[s, k], col_scale[s, k])
        gath[s, p], gath_scale[s, p] = encoded(total)
        for k in range(1, n_rows):
            gath_copy(s, k).start()

    def finish_diagonal(s):
        for k in range(1, n_rows):
            gath_wait(s, k)
        for k in range(n_rows):
            part_of = slice(k * seg, (k + 1) * seg)
            g_ref[s, part_of] = d_ref[s, part_of] + decoded(gath[s, k], gath_scale[s, k])

    def after(s, total):
        with scope(f"line{s}"):
            line_start(s, False)
        with scope(f"diag{s}"):
            diagonal_term(s, total)
            plane_start(s)

    with scope("frompair"):
        for s in range(nodes):
            for u in range(SUB):
                own_from_pair(s, u)
    steps = []
    for s in range(nodes - 1):
        for u in range(SUB):
            steps.append((own_from_x, s, u))
        for u in range(SUB):
            steps.append((others_from_hi, s, u))
    k = 0
    for step, s, u in steps:
        with scope(f"choose{k}"):
            while k < STRIPS * (steps.index((step, s, u)) + 1) // (len(steps) + 1):
                choose(k)
                k += 1
        with scope(f"{step.__name__}{s}{u}"):
            step(s, u)
    with scope("chooserest"):
        for k in range(k, STRIPS):
            choose(k)
    for s in range(nodes - 1):
        with scope(f"own{s + 1}a"):
            own_from_x(s + 1, 0)
        with scope(f"rest{s}"):
            rest(s)
        with scope(f"mult{s}"):
            total = multiply(s)
        with scope(f"own{s + 1}b"):
            for u in range(1, SUB):
                own_from_x(s + 1, u)
        after(s, total)
    last = nodes - 1
    with scope("others1"):
        for u in range(SUB):
            others_from_hi(last, u)
    with scope("rest1"):
        rest(last)
    with scope("mult1"):
        total = multiply(last)
    after(last, total)
    for s in range(nodes):
        with scope(f"relayA{s}"):
            relay(s, True)
        with scope(f"colstart{s}"):
            col_start(s)
            line_start(s, True)
        with scope(f"relayB{s}"):
            relay(s, False)
    for s in range(nodes):
        with scope(f"gathstart{s}"):
            gath_start(s)
    for s in range(nodes):
        with scope(f"finish{s}"):
            line_finish(s)
    with scope("drain"):
        for s in range(nodes):
            drain_blocks(s)
            line_drain(s)
            for k in range(1, n_rows):
                plane_copy(s, k).wait_send()
            for k in range(1, n_cols):
                col_copy(s, k).wait_send()
    for s in range(nodes):
        with scope(f"findiag{s}"):
            finish_diagonal(s)
    for s in range(nodes):
        for k in range(1, n_rows):
            gath_copy(s, k).wait_send()


def on_device(inverse, panel, structure, diag_inverse):
    n_rows = lax.axis_size("prow")
    n_cols = lax.axis_size("pcol")
    rows_local, block, cols_local, _ = inverse.shape
    nodes, _, _, width = panel.shape
    ratio = n_rows // n_cols
    piece = block // n_cols
    seg = width // n_rows
    strip = block // STRIPS

    vmem = pl.BlockSpec(memory_space=pltpu.VMEM)
    hbm = pl.BlockSpec(memory_space=pltpu.HBM)
    f32, bf16, i16 = jnp.float32, jnp.bfloat16, jnp.int16
    dma = pltpu.SemaphoreType.DMA
    sends = ratio - 1 + n_cols // 2 - 1 + ratio
    return pl.pallas_call(
        functools.partial(selected, n_rows, n_cols),
        out_shape=(
            jax.ShapeDtypeStruct((nodes, rows_local, piece, width), bf16),
            jax.ShapeDtypeStruct((nodes, width, width), f32),
        ),
        in_specs=[hbm, hbm, hbm, vmem],
        out_specs=(vmem, vmem),
        scratch_shapes=[
            pltpu.SMEM(structure.shape, jnp.int32),
            tuple(pltpu.VMEM(panel.shape[1:], bf16) for _ in range(nodes)),
            tuple(pltpu.VMEM((rows_local, strip, *inverse.shape[2:]), bf16) for _ in range(STRIPS)),
            pltpu.VMEM((nodes, block // 128, strip * cols_local, 128), f32),
            pltpu.VMEM((nodes, ratio, block, block), bf16),
            pltpu.VMEM((nodes, block, width), bf16),
            pltpu.VMEM((nodes, ratio, block, width), bf16),
            pltpu.VMEM((nodes, n_cols, piece, width), f32),
            pltpu.VMEM((nodes, n_cols, piece, width), i16),
            pltpu.VMEM((nodes, n_cols, piece, width), i16),
            pltpu.VMEM((nodes, n_cols, 1, width), f32),
            pltpu.VMEM((nodes, n_cols, 1, width), f32),
            pltpu.VMEM((nodes, n_rows, seg, width), f32),
            pltpu.VMEM((nodes, n_rows, seg, width), i16),
            pltpu.VMEM((nodes, 1, width), f32),
            pltpu.VMEM((nodes, n_rows, seg, width), i16),
            pltpu.VMEM((nodes, n_rows, 1, width), f32),
            pltpu.VMEM((nodes, n_cols, seg, width), i16),
            pltpu.VMEM((nodes, n_cols, 1, width), f32),
            pltpu.VMEM((nodes, n_rows, seg, width), i16),
            pltpu.VMEM((nodes, n_rows, 1, width), f32),
            dma, dma((nodes,)), dma((STRIPS,)),
            dma((nodes, 2 * SUB, sends)), dma((nodes, ratio, 2 * SUB)),
            dma((2, nodes, n_cols)), dma((2, nodes, n_cols)),
            dma((2, nodes, n_cols)), dma((2, nodes, n_cols)),
            dma((2, nodes, n_rows)), dma((2, nodes, n_rows)),
            dma((2, nodes, n_cols)), dma((2, nodes, n_cols)),
            dma((2, nodes, n_rows)), dma((2, nodes, n_rows)),
        ],
        compiler_params=pltpu.CompilerParams(
            collective_id=0, has_side_effects=True, vmem_limit_bytes=50 * 1024 * 1024
        ),
        name="selected_inverse",
    )(structure, inverse, panel, diag_inverse)


def solution(mesh):
    placed = (P(None, "prow", None, "pcol"), P(None, None, "prow", None), P(), P())
    return jax.shard_map(
        on_device,
        mesh=mesh,
        in_specs=placed,
        out_specs=(P(None, None, ("prow", "pcol"), None), P()),
        check_vma=False,
    )
```

time: 57 us -> 45.2 us (0.79)
  the two profiles are of different devices: /device:TPU:9 before, /device:TPU:0 now
where the time goes in v1:
time: 45.2 us; the launch traced here: 45 us
  Pallas kernels  39.4 us (87%)
  local copies, waits for them, and re-layouts  4.89 us (11%)
  between operations  0.65 us (1%)
    pallas_call x1, Pallas kernels, on_device(): pl.pallas_call(functools.partial(selected, n_rows, n_cols), out_shape=(ja...  39.4 us
    unnamed x8, local copies, waits for them, and re-layouts  4.89 us

profile of v1, /device:TPU:0, one launch (start us, length us, event | category | flops | bytes accessed | tf_op | source)
XLA Modules:
  0.0 45.0 jit_solution(13563687787280991690)
XLA Ops:
  0.6 0.0 copy-start
  0.6 1.6 %copy-done = bf16[2,4,512,256]{3,2,1,0:T(8,128)(2,1)S(1)} copy-done((bf16[2,4,512,256]{3,2,1,0:T(8,128)(2,1)S(1)}, bf16[2,4,512,256]{3,2,1,0:T(8,128)(2,1)}, u32[]{:S(2)}) %copy-start) | copy-done | bytes 2097176
  2.2 0.0 copy-start.1
  2.2 1.0 %copy-done.1 = f32[2,256,256]{2,1,0:T(8,128)S(1)} copy-done((f32[2,256,256]{2,1,0:T(8,128)S(1)}, f32[2,256,256]{2,1,0:T(8,128)}, u32[]{:S(2)}) %copy-start.1) | copy-done | bytes 524312
  3.3 0.0 copy-start.2
  3.3 0.7 %copy-done.2 = s32[2,8]{1,0:T(2,128)S(1)} copy-done((s32[2,8]{1,0:T(2,128)S(1)}, s32[2,8]{1,0:T(2,128)}, u32[]{:S(2)}) %copy-start.2) | copy-done | bytes 88
  3.9 39.4 %selected_inverse.1 = (bf16[2,4,128,256]{3,2,1,0:T(8,128)(2,1)S(1)}, f32[2,256,256]{2,1,0:T(8,128)S(1)}) custom-call(s32[2,8]{1,0:T(2,128)S(1)} %copy-done.2, bf16[4,512,8,512]{3,2,1,0:T(8,128)(2,1)} %inverse_ref.1, bf16[2,4,512,256]{3,2,1,0:T(8,128)(2,1)S(1)} %copy-done, f32[2,256,256]{2,1,0:T(8,128)S(1)} %copy-done.1), custom_call_target="tpu_custom_call" | custom-call | tf_op jit(solution)/shard_map/selected_inverse/pallas_call | solution.py:492
  43.4 0.8 %copy.8 = bf16[2,4,128,256]{3,2,1,0:T(8,128)(2,1)} copy(bf16[2,4,128,256]{3,2,1,0:T(8,128)(2,1)S(1)} %get-tuple-element.4) | data formatting | bytes 1048576
  44.2 0.8 %copy.9 = f32[2,256,256]{2,1,0:T(8,128)} copy(f32[2,256,256]{2,1,0:T(8,128)S(1)} %get-tuple-element.5) | data formatting | bytes 1048576
Async XLA Ops:
  0.6 1.6 %copy-start = (bf16[2,4,512,256]{3,2,1,0:T(8,128)(2,1)S(1)}, bf16[2,4,512,256]{3,2,1,0:T(8,128)(2,1)}, u32[]{:S(2)}) copy-start(bf16[2,4,512,256]{3,2,1,0:T(8,128)(2,1)} %panel_ref.1) | copy-start | bytes 6291460
  2.2 1.0 %copy-start.1 = (f32[2,256,256]{2,1,0:T(8,128)S(1)}, f32[2,256,256]{2,1,0:T(8,128)}, u32[]{:S(2)}) copy-start(f32[2,256,256]{2,1,0:T(8,128)} %d_ref.1) | copy-start | bytes 1572868
  3.3 0.7 %copy-start.2 = (s32[2,8]{1,0:T(2,128)S(1)}, s32[2,8]{1,0:T(2,128)}, u32[]{:S(2)}) copy-start(s32[2,8]{1,0:T(2,128)} %structure_hbm.1) | copy-start | bytes 196

commit v2 on v1

v2 whole, which is shorter than its diff:
```python
import functools

import jax
import jax.numpy as jnp
from jax import lax
from jax.experimental import pallas as pl
from jax.experimental.pallas import tpu as pltpu
from jax.sharding import PartitionSpec as P

MESH = pl.DeviceIdType.MESH
SUB = 4
STRIPS = 8
AHEAD = 4
FULL = 32700.0


def remote(src, dst, send, recv, p, q):
    return pltpu.make_async_remote_copy(
        src_ref=src, dst_ref=dst, send_sem=send, recv_sem=recv, device_id=(p, q), device_id_type=MESH
    )


def scope(name):
    return jax.named_scope(name)


def find_row(structure_ref, s, residue, n_rows, divisor):
    found = jnp.int32(0)
    for i in range(structure_ref.shape[1]):
        value = structure_ref[s, i]
        found = found + jnp.where(value % n_rows == residue, value // divisor, 0)
    return found


def selected(
    n_rows, n_cols, structure_hbm, inverse_ref, panel_ref, y_out, g_out, scale_out,
    structure_ref, y_ref, own, own_scale, panel_buf, raw, wide, a_ref, l_ref, l_buf, part,
    right_buf, left_buf, right_scale, left_scale,
    term, term_buf, term_scale, plane_buf, plane_scale, col_own, col_own_scale, col_buf, col_scale,
    s_sem, n_sem, a_sem, o_sem,
    l_send, l_recv, r_send, f_send, r_recv, p_send, p_recv, c_send, c_recv, g_send, g_recv,
):
    p = lax.axis_index("prow")
    q = lax.axis_index("pcol")
    nodes, ratio, block, width = l_buf.shape
    rows_local, _, cols_local, _ = inverse_ref.shape
    piece = block // n_cols
    seg = width // n_rows
    chunk = block // (2 * SUB)
    strip = block // STRIPS
    hi = p // n_cols
    lo = p % n_cols
    t = jnp.int32(0)
    bit = 1
    while bit < n_cols:
        t = t + bit * (((lo // bit) + (q // bit)) % 2)
        bit *= 2
    pair = p + 1 - 2 * (p % 2)

    def beside(j):
        lo2 = jnp.int32(0)
        b = 1
        while b < n_cols:
            lo2 = lo2 + b * (((lo // b) + (2 * j // b)) % 2)
            b *= 2
        return hi * n_cols + lo2

    structure_copy = pltpu.make_async_copy(structure_hbm, structure_ref, s_sem)
    structure_copy.start()
    panel_copies = [pltpu.make_async_copy(panel_ref.at[s], panel_buf[s], n_sem.at[s]) for s in range(nodes)]
    for copy in panel_copies:
        copy.start()

    def strip_copy(k):
        part_of = pl.ds(k * strip, strip)
        return pltpu.make_async_copy(inverse_ref.at[:, part_of], raw[k], a_sem.at[k % AHEAD])

    barrier = pltpu.get_barrier_semaphore()
    for k in range(1, n_rows):
        pl.semaphore_signal(barrier, inc=1, device_id=((p + k) % n_rows, q), device_id_type=MESH)
    for k in range(1, n_cols):
        pl.semaphore_signal(barrier, inc=1, device_id=(p, (q + k) % n_cols), device_id_type=MESH)

    def find(s, residue, divisor):
        return find_row(structure_ref, s, residue, n_rows, divisor)

    with scope("pickl"):
        structure_copy.wait()
        row = [find(s, p, n_rows) for s in range(nodes)]
        cols = [[find(s, h * n_cols + q, n_cols) for h in range(ratio)] for s in range(nodes)]
        for s in range(nodes):
            panel_copies[s].wait()
            l_ref[s] = panel_buf[s][row[s]]
        for k in range(AHEAD):
            strip_copy(k).start()

    with scope("barrier"):
        pl.semaphore_wait(barrier, n_rows + n_cols - 2)

    def rows(c):
        return pl.ds(pl.multiple_of(c * chunk, chunk), chunk)

    def l_slot(s, h, c):
        return l_buf.at[s, h, rows(c)]

    def to_peer_hi(s, c, k, src):
        return remote(src, l_slot(s, hi, c), l_send.at[s, k - 1], l_recv.at[s, hi, c % SUB],
                      (p + k * n_cols) % n_rows, q)

    def to_x(s, c, j, src):
        return remote(src, l_slot(s, hi, c), l_send.at[s, ratio - 1 + j - 1], l_recv.at[s, hi, c % SUB],
                      beside(j), q)

    def to_pair(s, c, k, src):
        h = (hi + k) % ratio
        return remote(src, l_slot(s, h, c), l_send.at[s, ratio - 1 + n_cols // 2 - 1 + k],
                      l_recv.at[s, h, SUB], pair, q)

    def hand_over(s, c):
        return remote(l_ref.at[s, rows(c)], l_slot(s, hi, c), l_send.at[s, 2 * ratio - 1 + n_cols // 2 - 1],
                      l_recv.at[s, hi, c % SUB], pair, q)

    def l_arrived(s, c, h):
        remote(l_slot(s, h, c), l_slot(s, h, c), l_send.at[s, 0], l_recv.at[s, h, c % SUB], pair, q).wait_recv()

    def half(s, h):
        return l_buf.at[s, h, pl.ds(0, SUB * chunk)]

    def half_arrived(s, h):
        remote(half(s, h), half(s, h), l_send.at[s, 0], l_recv.at[s, h, SUB], pair, q).wait_recv()

    def half_sent(s, i):
        remote(half(s, 0), half(s, 0), l_send.at[s, i], l_recv.at[s, 0, 0], pair, q).wait_send()

    owner = t == 0
    source_chip = t < 2
    core = p % 2

    def mine(u):
        return core * SUB + u

    def other(u):
        return (1 - core) * SUB + u

    @pl.when(owner)
    def _():
        for s in range(nodes):
            for u in range(SUB):
                hand_over(s, other(u)).start()
            for u in range(SUB):
                src = l_ref.at[s, rows(mine(u))]
                for j in range(1, n_cols // 2):
                    to_x(s, mine(u), j, src).start()
                for k in range(1, ratio):
                    to_peer_hi(s, mine(u), k, src).start()
            for u in range(SUB):
                to_pair(s, mine(u), 0, l_ref.at[s, rows(mine(u))]).start()
        for s in range(nodes):
            l_buf[s, hi] = l_ref[s]

    def own_from_pair(s, u):
        c = mine(u)

        @pl.when(t == 1)
        def _():
            l_arrived(s, c, hi)
            for j in range(1, n_cols // 2):
                to_x(s, c, j, l_slot(s, hi, c)).start()
            for k in range(1, ratio):
                to_peer_hi(s, c, k, l_slot(s, hi, c)).start()

    def own_from_x(s, u):
        c = mine(u)

        @pl.when(jnp.logical_not(source_chip))
        def _():
            l_arrived(s, c, hi)
            for k in range(1, ratio):
                to_peer_hi(s, c, k, l_slot(s, hi, c)).start()
            to_pair(s, c, 0, l_slot(s, hi, c)).start()

    def others_from_hi(s, u):
        c = mine(u)
        for k in range(1, ratio):
            l_arrived(s, c, (hi + k) % ratio)
            to_pair(s, c, k, l_slot(s, (hi + k) % ratio, c)).start()

    def rest_own(s):
        @pl.when(jnp.logical_not(owner))
        def _():
            half_arrived(s, hi)

    def rest(s):
        for k in range(1, ratio):
            half_arrived(s, (hi + k) % ratio)

    def drain_blocks(s):
        for k in range(1, ratio):
            half_sent(s, k - 1)
            half_sent(s, ratio - 1 + n_cols // 2 - 1 + k)

        @pl.when(source_chip)
        def _():
            for j in range(1, n_cols // 2):
                half_sent(s, ratio - 1 + j - 1)

        @pl.when(t != 1)
        def _():
            half_sent(s, ratio - 1 + n_cols // 2 - 1)

        @pl.when(owner)
        def _():
            half_sent(s, 2 * ratio - 1 + n_cols // 2 - 1)

    def choose(k):
        strip_copy(k).wait()
        if k + AHEAD < STRIPS:
            strip_copy(k + AHEAD).start()
        for s in range(nodes):
            for b in range(block // 128):
                lanes = raw[k][row[s], :, :, b * 128:(b + 1) * 128].astype(jnp.float32)
                wide[s, b] = lanes.reshape(strip * cols_local, 128)
            for h in range(ratio):
                for b in range(block // 128):
                    a_ref[s, h, k * strip:(k + 1) * strip, b * 128:(b + 1) * 128] = wide[
                        s, b, pl.ds(cols[s][h], strip, stride=cols_local)
                    ].astype(jnp.bfloat16)

    def multiply_own(s):
        rest_own(s)
        total = jnp.dot(a_ref[s, hi], l_buf[s, hi], preferred_element_type=jnp.float32)
        for d in range(n_cols):
            part[s, d] = total[d * piece:(d + 1) * piece]

    def multiply(s):
        h = [(hi + k) % ratio for k in range(1, ratio)]
        total = jnp.dot(a_ref[s, h[0]], l_buf[s, h[0]], preferred_element_type=jnp.float32)
        for k in h[1:]:
            total += jnp.dot(a_ref[s, k], l_buf[s, k], preferred_element_type=jnp.float32)
        total = jnp.concatenate([part[s, d] + total[d * piece:(d + 1) * piece] for d in range(n_cols)], axis=0)
        for d in range(n_cols):
            part[s, d] = total[d * piece:(d + 1) * piece]
        return total

    def encoded(value):
        largest = jnp.maximum(jnp.max(jnp.abs(value), axis=0, keepdims=True), 1e-30)
        whole = jnp.floor(value * (FULL / largest) + 0.5).astype(jnp.int32).astype(jnp.int16)
        return whole, largest * (1.0 / FULL)

    def decoded(whole, scale):
        return whole.astype(jnp.int32).astype(jnp.float32) * scale

    def diagonal_term(s, total):
        high = total.astype(jnp.bfloat16)
        low = (total - high.astype(jnp.float32)).astype(jnp.bfloat16)
        over_rows = (((0,), (0,)), ((), ()))
        product = lax.dot_general(l_ref[s], high, over_rows, preferred_element_type=jnp.float32)
        product += lax.dot_general(l_ref[s], low, over_rows, preferred_element_type=jnp.float32)
        whole, scale = encoded(product)
        term_scale[s] = scale
        for k in range(n_rows):
            term[s, k] = product[k * seg:(k + 1) * seg]
            term_buf[s, k] = whole[k * seg:(k + 1) * seg]

    class both:
        def __init__(self, src, src_scale, dst, dst_scale, send, recv, send_at, recv_at, to_p, to_q):
            self.copies = [
                remote(src, dst, send.at[(0, *send_at)], recv.at[(0, *recv_at)], to_p, to_q),
                remote(src_scale, dst_scale, send.at[(1, *send_at)], recv.at[(1, *recv_at)], to_p, to_q),
            ]

        def start(self):
            for copy in self.copies:
                copy.start()

        def wait_send(self):
            for copy in self.copies:
                copy.wait_send()

        def wait_recv(self):
            for copy in self.copies:
                copy.wait_recv()

    def right_copy(s, d):
        return both(right_buf.at[s, d], right_scale.at[s, d], right_buf.at[s, d], right_scale.at[s, d],
                    r_send, r_recv, (s,), (s, d), p, (q + 1) % n_cols)

    def left_copy(s, d, at):
        last = jnp.where(at == d, n_cols, d)
        return both(left_buf.at[s, d], left_scale.at[s, d], left_buf.at[s, d], left_scale.at[s, d],
                    f_send, r_recv, (s,), (s, last), p, (q + n_cols - 1) % n_cols)

    def right_send(s, d, value):
        right_buf[s, d], right_scale[s, d] = encoded(value)
        right_copy(s, d).start()

    def left_send(s, d, value):
        left_buf[s, d], left_scale[s, d] = encoded(value)
        left_copy(s, d, q - 1).start()

    def line_start(s, nearest):
        @pl.when(q == 0)
        def _():
            for d in ((1,) if nearest else range(n_cols - 1, 1, -1)):
                right_send(s, d, part[s, d])

        @pl.when(q == n_cols - 1)
        def _():
            for d in ((n_cols - 2,) if nearest else range(n_cols - 2)):
                left_send(s, d, part[s, d])

    def relay_right(s):
        for d in range(n_cols - 1, 1, -1):
            @pl.when(jnp.logical_and(q > 0, q < d))
            def _():
                right_copy(s, d).wait_recv()
                right_send(s, d, decoded(right_buf[s, d], right_scale[s, d]) + part[s, d])

    def relay_left(s):
        for e in range(n_cols - 2):
            @pl.when(jnp.logical_and(q < n_cols - 1, q > e))
            def _():
                left_copy(s, e, q).wait_recv()
                left_send(s, e, decoded(left_buf[s, e], left_scale[s, e]) + part[s, e])

    left_half = 2 * q < n_cols - 1

    def relay(s, first):
        @pl.when(left_half)
        def _():
            (relay_right if first else relay_left)(s)

        @pl.when(jnp.logical_not(left_half))
        def _():
            (relay_left if first else relay_right)(s)

    def near(s, source):
        @pl.when(source_chip if source else jnp.logical_not(source_chip))
        def _():
            line_start(s, True)

    def relay_early(s, source):
        @pl.when(source_chip if source else jnp.logical_not(source_chip))
        def _():
            relay(s, True)

    def line_finish(s):
        @pl.when(q > 0)
        def _():
            right_copy(s, q).wait_recv()
            part[s, q] = part[s, q] + decoded(right_buf[s, q], right_scale[s, q])

        @pl.when(q < n_cols - 1)
        def _():
            left_copy(s, q, q).wait_recv()
            part[s, q] = part[s, q] + decoded(left_buf[s, q], left_scale[s, q])

        y_ref[s] = (-part[s, q]).astype(jnp.bfloat16)
        pltpu.make_async_copy(y_ref.at[s], y_out.at[s], o_sem.at[s, 0]).start()

    def line_drain(s):
        for at in range(n_cols):
            @pl.when(q == at)
            def _():
                for n, buf, scale, send in ((n_cols - 1 - at, right_buf, right_scale, r_send),
                                            (at, left_buf, left_scale, f_send)):
                    if n:
                        some = pl.ds(0, n)
                        both(buf.at[s, some], scale.at[s, some], buf.at[s, some], scale.at[s, some],
                             send, r_recv, (s,), (s, 0), p, (q + 1) % n_cols).wait_send()

    def plane_copy(s, k):
        to = (p + k) % n_rows
        return both(term_buf.at[s, to], term_scale.at[s], plane_buf.at[s, n_rows - k], plane_scale.at[s, n_rows - k],
                    p_send, p_recv, (s,), (s,), to, q)

    def col_copy(s, k):
        to = (q + k) % n_cols
        return both(col_own.at[s], col_own_scale.at[s], col_buf.at[s, q], col_scale.at[s, q],
                    c_send, c_recv, (s,), (s,), p, to)

    def gath_copy(s, k):
        to = (p + k) % n_rows
        return both(own.at[s], own_scale.at[s], g_out.at[s, p], scale_out.at[s, p],
                    g_send, g_recv, (s,), (s,), to, q)

    def all_of(s, n, buf, scale, send, recv):
        some = pl.ds(0, n - 1)
        return both(buf.at[s, some], scale.at[s, some], buf.at[s, some], scale.at[s, some],
                    send, recv, (s,), (s,), pair, q)

    def plane_all(s):
        return all_of(s, n_rows, plane_buf, plane_scale, p_send, p_recv)

    def col_all(s):
        return all_of(s, n_cols, col_buf, col_scale, c_send, c_recv)

    def gath_all(s):
        return all_of(s, n_rows, g_out, scale_out, g_send, g_recv)

    def own_copies(s):
        return [pltpu.make_async_copy(own.at[s], g_out.at[s, p], o_sem.at[s, 1]),
                pltpu.make_async_copy(own_scale.at[s], scale_out.at[s, p], o_sem.at[s, 2])]

    def plane_start(s):
        for k in range(1, n_rows):
            plane_copy(s, k).start()

    def col_start(s):
        total = term[s, p]
        plane_all(s).wait_recv()
        for k in range(1, n_rows):
            total = total + decoded(plane_buf[s, k], plane_scale[s, k])
        col_own[s], col_own_scale[s] = encoded(total)
        for k in range(1, n_cols):
            col_copy(s, k).start()

    def gath_start(s):
        mine_own = decoded(col_own[s], col_own_scale[s])
        col_all(s).wait_recv()
        total = jnp.zeros_like(mine_own)
        for k in range(n_cols):
            total = total + jnp.where(q == k, mine_own, decoded(col_buf[s, k], col_scale[s, k]))
        own[s], own_scale[s] = encoded(total)
        for k in range(1, n_rows):
            gath_copy(s, k).start()
        for copy in own_copies(s):
            copy.start()

    def finish_diagonal(s):
        pltpu.make_async_copy(y_ref.at[s], y_out.at[s], o_sem.at[s, 0]).wait()
        for copy in own_copies(s):
            copy.wait()
        gath_all(s).wait_recv()

    def after(s, total):
        with scope(f"line{s}"):
            line_start(s, False)
            near(s, True)
        with scope(f"diag{s}"):
            diagonal_term(s, total)
            plane_start(s)

    with scope("frompair"):
        for s in range(nodes):
            for u in range(SUB):
                own_from_pair(s, u)
    def flow(s):
        order = []
        for u in range(SUB):
            order.append((others_from_hi, s, u))
            if s + 1 < nodes:
                order.append((own_from_x, s + 1, u))
        return order

    first = [(own_from_x, 0, u) for u in range(SUB)] + flow(0)
    chosen = 0
    for i, (step, s, u) in enumerate(first):
        ready = STRIPS if i + 1 == len(first) else min(STRIPS, 2 + i)
        with scope(f"choose{i}"):
            for k in range(chosen, ready):
                choose(k)
            chosen = ready
        if i + 2 == len(first):
            with scope("own0"):
                multiply_own(0)
        with scope(f"{step.__name__}{s}{u}"):
            step(s, u)
    for s in range(nodes):
        with scope(f"rest{s}"):
            rest(s)
        with scope(f"mult{s}"):
            total = multiply(s)
        after(s, total)
        if s + 1 < nodes:
            order = flow(s + 1)
            for i, (step, to, u) in enumerate(order):
                if 2 * i == len(order):
                    with scope(f"own{s + 1}"):
                        multiply_own(s + 1)
                with scope(f"flow{s + 1}{i}"):
                    step(to, u)
            with scope(f"relayA{s}"):
                relay_early(s, True)
    for s in range(nodes):
        if s + 1 < nodes:
            with scope(f"relayT{s}"):
                relay_early(s, False)
        with scope(f"colstart{s}"):
            col_start(s)
            near(s, False)
        if s + 1 == nodes:
            with scope(f"relayA{s}"):
                relay(s, True)
            for i in range(nodes - 1):
                with scope(f"gathstart{i}"):
                    gath_start(i)
        with scope(f"relayB{s}"):
            relay(s, False)
    with scope(f"gathstart{nodes - 1}"):
        gath_start(nodes - 1)
    for s in range(nodes):
        with scope(f"finish{s}"):
            line_finish(s)
    with scope("drain"):
        for s in range(nodes):
            drain_blocks(s)
            line_drain(s)
            plane_all(s).wait_send()
            col_all(s).wait_send()
    for s in range(nodes):
        with scope(f"findiag{s}"):
            finish_diagonal(s)
    for s in range(nodes):
        with scope("sent"):
            gath_all(s).wait_send()


def put_out(structure_ref, y_ref, whole_ref, scale_ref, d_ref, off_ref, out_ref, off_buf, out_buf, sem):
    nodes, n_rows, seg, _ = whole_ref.shape
    rows_local = off_ref.shape[1]
    copies = []
    for s in range(nodes):
        row = find_row(structure_ref, s, lax.axis_index("prow"), n_rows, n_rows)
        value = y_ref[s]
        for r in range(rows_local):
            off_buf[s, r] = jnp.where(row == r, value, jnp.zeros_like(value))
        copies.append(pltpu.make_async_copy(off_buf.at[s], off_ref.at[s], sem.at[0, s]))
        copies[-1].start()
        for k in range(n_rows):
            term = whole_ref[s, k].astype(jnp.int32).astype(jnp.float32) * scale_ref[s, k]
            out_buf[s, k * seg:(k + 1) * seg] = d_ref[s, k * seg:(k + 1) * seg] + term
        copies.append(pltpu.make_async_copy(out_buf.at[s], out_ref.at[s], sem.at[1, s]))
        copies[-1].start()
    for copy in copies:
        copy.wait()


def on_device(inverse, panel, structure, diag_inverse):
    n_rows = lax.axis_size("prow")
    n_cols = lax.axis_size("pcol")
    rows_local, block, cols_local, _ = inverse.shape
    nodes, _, _, width = panel.shape
    ratio = n_rows // n_cols
    piece = block // n_cols
    seg = width // n_rows
    strip = block // STRIPS

    vmem = pl.BlockSpec(memory_space=pltpu.VMEM)
    hbm = pl.BlockSpec(memory_space=pltpu.HBM)
    f32, bf16, i16 = jnp.float32, jnp.bfloat16, jnp.int16
    dma = pltpu.SemaphoreType.DMA
    sends = ratio + n_cols // 2 - 1 + ratio
    operands = [pltpu.with_memory_space_constraint(x, pltpu.HBM) for x in (structure, inverse, panel)]
    anywhere = pl.BlockSpec(memory_space=pl.ANY)
    smem = pl.BlockSpec(memory_space=pltpu.SMEM)
    pieces, whole, scale = pl.pallas_call(
        functools.partial(selected, n_rows, n_cols),
        out_shape=(
            jax.ShapeDtypeStruct((nodes, piece, width), bf16),
            jax.ShapeDtypeStruct((nodes, n_rows, seg, width), i16),
            jax.ShapeDtypeStruct((nodes, n_rows, 1, width), f32),
        ),
        in_specs=[hbm] * 3,
        out_specs=(anywhere, anywhere, anywhere),
        scratch_shapes=[
            pltpu.SMEM(structure.shape, jnp.int32),
            pltpu.VMEM((nodes, piece, width), bf16),
            pltpu.VMEM((nodes, seg, width), i16),
            pltpu.VMEM((nodes, 1, width), f32),
            tuple(pltpu.VMEM(panel.shape[1:], bf16) for _ in range(nodes)),
            tuple(pltpu.VMEM((rows_local, strip, *inverse.shape[2:]), bf16) for _ in range(STRIPS)),
            pltpu.VMEM((nodes, block // 128, strip * cols_local, 128), f32),
            pltpu.VMEM((nodes, ratio, block, block), bf16),
            pltpu.VMEM((nodes, block, width), bf16),
            pltpu.VMEM((nodes, ratio, block, width), bf16),
            pltpu.VMEM((nodes, n_cols, piece, width), f32),
            pltpu.VMEM((nodes, n_cols, piece, width), i16),
            pltpu.VMEM((nodes, n_cols, piece, width), i16),
            pltpu.VMEM((nodes, n_cols, 1, width), f32),
            pltpu.VMEM((nodes, n_cols, 1, width), f32),
            pltpu.VMEM((nodes, n_rows, seg, width), f32),
            pltpu.VMEM((nodes, n_rows, seg, width), i16),
            pltpu.VMEM((nodes, 1, width), f32),
            pltpu.VMEM((nodes, n_rows, seg, width), i16),
            pltpu.VMEM((nodes, n_rows, 1, width), f32),
            pltpu.VMEM((nodes, seg, width), i16),
            pltpu.VMEM((nodes, 1, width), f32),
            pltpu.VMEM((nodes, n_cols, seg, width), i16),
            pltpu.VMEM((nodes, n_cols, 1, width), f32),
            dma, dma((nodes,)), dma((AHEAD,)), dma((nodes, 3)),
            dma((nodes, sends)), dma((nodes, ratio, SUB + 1)),
            dma((2, nodes)), dma((2, nodes)), dma((2, nodes, n_cols + 1)),
            *(dma((2, nodes)) for _ in range(6)),
        ],
        compiler_params=pltpu.CompilerParams(
            collective_id=0, has_side_effects=True, vmem_limit_bytes=50 * 1024 * 1024
        ),
        name="selected_inverse",
    )(*operands)
    return pl.pallas_call(
        put_out,
        out_shape=(
            jax.ShapeDtypeStruct((nodes, rows_local, piece, width), bf16),
            jax.ShapeDtypeStruct(diag_inverse.shape, f32),
        ),
        in_specs=[smem, vmem, vmem, vmem, vmem],
        out_specs=(hbm, hbm),
        scratch_shapes=[
            pltpu.VMEM((nodes, rows_local, piece, width), bf16),
            pltpu.VMEM(diag_inverse.shape, f32),
            dma((2, nodes)),
        ],
        compiler_params=pltpu.CompilerParams(vmem_limit_bytes=4 * 1024 * 1024),
        name="put_out",
    )(structure, pieces, whole, scale, diag_inverse)


def solution(mesh):
    placed = (P(None, "prow", None, "pcol"), P(None, None, "prow", None), P(), P())
    return jax.shard_map(
        on_device,
        mesh=mesh,
        in_specs=placed,
        out_specs=(P(None, None, ("prow", "pcol"), None), P()),
        check_vma=False,
    )
```

time: 45.2 us -> 35.7 us (0.79)
  local copies, waits for them, and re-layouts: 4.89 us -> 0.01 us
  Pallas kernels: 39.4 us -> 34.8 us
    pallas_call x1, Pallas kernels: 39.4 us -> 33.2 us  [on_device(): pl.pallas_call(functools.partial(selected, n_rows, n_cols), out_shape=(ja...]
    unnamed x8 -> x4, local copies, waits for them, and re-layouts: 4.89 us -> 0.01 us
    pallas_call x0 -> x1, Pallas kernels: none -> 1.62 us  [on_device(): pl.pallas_call(put_out, out_shape=(jax.ShapeDtypeStruct((nodes, rows_loca...]
where the time goes in v2:
time: 35.7 us; the launch traced here: 35.5 us
  Pallas kernels  34.8 us (97%)
  between operations  0.67 us (2%)
    pallas_call x1, Pallas kernels, on_device(): pl.pallas_call(functools.partial(selected, n_rows, n_cols), out_shape=(ja...  33.2 us
    pallas_call x1, Pallas kernels, on_device(): pl.pallas_call(put_out, out_shape=(jax.ShapeDtypeStruct((nodes, rows_loca...  1.62 us

profile of v2, /device:TPU:0, one launch (start us, length us, event | category | flops | bytes accessed | tf_op | source)
XLA Modules:
  0.0 35.5 jit_solution(13538954859363152058)
XLA Ops:
  0.6 0.0 copy-start.1
  0.6 0.0 copy-start
  0.7 33.2 %selected_inverse.1 = (bf16[2,128,256]{2,1,0:T(8,128)(2,1)S(1)}, s16[2,8,32,256]{3,2,1,0:T(8,128)(2,1)S(1)}, f32[2,8,1,256]{3,2,1,0:T(1,128)S(1)}) custom-call(s32[2,8]{1,0:T(2,128)} %structure_ref.1, bf16[4,512,8,512]{3,2,1,0:T(8,128)(2,1)} %inverse_ref.1, bf16[2,4,512,256]{3,2,1,0:T(8,128)(2,1)} %panel_ref.1), custom_call_target="tpu_custom_call" | custom-call | tf_op jit(solution)/shard_map/selected_inverse/pallas_call | solution.py:557
  33.9 0.0 copy-done.1
  33.9 0.0 copy-done
  33.9 1.6 %put_out.1 = (bf16[2,4,128,256]{3,2,1,0:T(8,128)(2,1)}, f32[2,256,256]{2,1,0:T(8,128)}) custom-call(s32[2,8]{1,0:T(2,128)S(1)} %copy-done.1, bf16[2,128,256]{2,1,0:T(8,128)(2,1)S(1)} %get-tuple-element.5.y_ref, s16[2,8,32,256]{3,2,1,0:T(8,128)(2,1)S(1)} %get-tuple-element.6.whole_ref, f32[2,8,1,256]{3,2,1,0:T(1,128)S(1)} %get-tuple-element.7.scale_ref, ...), custom_call_target="tpu_custom_call" | custom-call | tf_op jit(solution)/shard_map/put_out/pallas_call | solution.py:601
Async XLA Ops:
  0.6 33.2 %copy-start.1 = (s32[2,8]{1,0:T(2,128)S(1)}, s32[2,8]{1,0:T(2,128)}, u32[]{:S(2)}) copy-start(s32[2,8]{1,0:T(2,128)} %structure_ref.1) | copy-start | bytes 196
  0.6 33.2 %copy-start = (f32[2,256,256]{2,1,0:T(8,128)S(1)}, f32[2,256,256]{2,1,0:T(8,128)}, u32[]{:S(2)}) copy-start(f32[2,256,256]{2,1,0:T(8,128)} %d_ref.1) | copy-start | bytes 1572868

commit v3 on v2

--- a/solution.py
+++ b/solution.py
@@ -25,19 +25,20 @@
 
 
 def find_row(structure_ref, s, residue, n_rows, divisor):
+    shift = divisor.bit_length() - 1
     found = jnp.int32(0)
     for i in range(structure_ref.shape[1]):
         value = structure_ref[s, i]
-        found = found + jnp.where(value % n_rows == residue, value // divisor, 0)
+        found = found + jnp.where((value & (n_rows - 1)) == residue, value >> shift, 0)
     return found
 
 
 def selected(
-    n_rows, n_cols, structure_hbm, inverse_ref, panel_ref, y_out, g_out, scale_out,
-    structure_ref, y_ref, own, own_scale, panel_buf, raw, wide, a_ref, l_ref, l_buf, part,
+    n_rows, n_cols, structure_hbm, inverse_ref, panel_ref, y_out, g_out, scale_out, mask_out,
+    structure_ref, mask, y_ref, own, own_scale, panel_buf, raw, wide, a_ref, l_ref, l_buf, part,
     right_buf, left_buf, right_scale, left_scale,
     term, term_buf, term_scale, plane_buf, plane_scale, col_own, col_own_scale, col_buf, col_scale,
-    s_sem, n_sem, a_sem, o_sem,
+    s_sem, m_sem, n_sem, a_sem, o_sem,
     l_send, l_recv, r_send, f_send, r_recv, p_send, p_recv, c_send, c_recv, g_send, g_recv,
 ):
     p = lax.axis_index("prow")
@@ -86,11 +87,9 @@
 
     with scope("pickl"):
         structure_copy.wait()
-        row = [find(s, p, n_rows) for s in range(nodes)]
-        cols = [[find(s, h * n_cols + q, n_cols) for h in range(ratio)] for s in range(nodes)]
-        for s in range(nodes):
-            panel_copies[s].wait()
-            l_ref[s] = panel_buf[s][row[s]]
+        row = [find(0, p, n_rows)]
+        panel_copies[0].wait()
+        l_ref[0] = panel_buf[0][row[0]]
         for k in range(AHEAD):
             strip_copy(k).start()
 
@@ -142,9 +141,14 @@
     def other(u):
         return (1 - core) * SUB + u
 
-    @pl.when(owner)
-    def _():
-        for s in range(nodes):
+    for s in range(nodes):
+        if s > 0:
+            row.append(find(s, p, n_rows))
+            panel_copies[s].wait()
+            l_ref[s] = panel_buf[s][row[s]]
+
+        @pl.when(owner)
+        def _():
             for u in range(SUB):
                 hand_over(s, other(u)).start()
             for u in range(SUB):
@@ -155,6 +159,16 @@
                     to_peer_hi(s, mine(u), k, src).start()
             for u in range(SUB):
                 to_pair(s, mine(u), 0, l_ref.at[s, rows(mine(u))]).start()
+
+    cols = [[find(s, h * n_cols + q, n_cols) for h in range(ratio)] for s in range(nodes)]
+    for s in range(nodes):
+        for r in range(rows_local):
+            mask[s, r] = jnp.broadcast_to(jnp.where(row[s] == r, 1.0, 0.0), mask.shape[2:])
+    mask_copy = pltpu.make_async_copy(mask, mask_out, m_sem)
+    mask_copy.start()
+
+    @pl.when(owner)
+    def _():
         for s in range(nodes):
             l_buf[s, hi] = l_ref[s]
 
@@ -309,15 +323,15 @@
             for d in ((n_cols - 2,) if nearest else range(n_cols - 2)):
                 left_send(s, d, part[s, d])
 
-    def relay_right(s):
-        for d in range(n_cols - 1, 1, -1):
+    def relay_right(s, some=slice(None)):
+        for d in range(n_cols - 1, 1, -1)[some]:
             @pl.when(jnp.logical_and(q > 0, q < d))
             def _():
                 right_copy(s, d).wait_recv()
                 right_send(s, d, decoded(right_buf[s, d], right_scale[s, d]) + part[s, d])
 
-    def relay_left(s):
-        for e in range(n_cols - 2):
+    def relay_left(s, some=slice(None)):
+        for e in range(n_cols - 2)[some]:
             @pl.when(jnp.logical_and(q < n_cols - 1, q > e))
             def _():
                 left_copy(s, e, q).wait_recv()
@@ -325,24 +339,24 @@
 
     left_half = 2 * q < n_cols - 1
 
-    def relay(s, first):
+    def relay(s, first, some=slice(None)):
         @pl.when(left_half)
         def _():
-            (relay_right if first else relay_left)(s)
+            (relay_right if first else relay_left)(s, some)
 
         @pl.when(jnp.logical_not(left_half))
         def _():
-            (relay_left if first else relay_right)(s)
+            (relay_left if first else relay_right)(s, some)
 
     def near(s, source):
         @pl.when(source_chip if source else jnp.logical_not(source_chip))
         def _():
             line_start(s, True)
 
-    def relay_early(s, source):
+    def relay_early(s, source, some=slice(None)):
         @pl.when(source_chip if source else jnp.logical_not(source_chip))
         def _():
-            relay(s, True)
+            relay(s, True, some)
 
     def line_finish(s):
         @pl.when(q > 0)
@@ -436,7 +450,9 @@
     def after(s, total):
         with scope(f"line{s}"):
             line_start(s, False)
-            near(s, True)
+            if s + 1 == nodes:
+                for i in range(nodes):
+                    near(i, True)
         with scope(f"diag{s}"):
             diagonal_term(s, total)
             plane_start(s)
@@ -482,27 +498,36 @@
                     step(to, u)
             with scope(f"relayA{s}"):
                 relay_early(s, True)
-    for s in range(nodes):
-        if s + 1 < nodes:
-            with scope(f"relayT{s}"):
-                relay_early(s, False)
+    last = nodes - 1
+    for s in range(last):
+        with scope(f"relayT{s}"):
+            relay_early(s, False)
+    for s in range(nodes):
         with scope(f"colstart{s}"):
             col_start(s)
-            near(s, False)
-        if s + 1 == nodes:
-            with scope(f"relayA{s}"):
-                relay(s, True)
-            for i in range(nodes - 1):
-                with scope(f"gathstart{i}"):
-                    gath_start(i)
-        with scope(f"relayB{s}"):
-            relay(s, False)
-    with scope(f"gathstart{nodes - 1}"):
-        gath_start(nodes - 1)
+        if s < last:
+            with scope(f"relayA{s + 1}"):
+                relay_early(s + 1, True)
+            with scope(f"relayB{s}"):
+                relay(s, False)
+    for s in range(nodes):
+        near(s, False)
+    with scope(f"relayT{last}"):
+        relay_early(last, False, slice(0, 1))
+    for s in range(last):
+        with scope(f"gathstart{s}"):
+            gath_start(s)
+    with scope(f"relayU{last}"):
+        relay_early(last, False, slice(1, None))
+    with scope(f"gathstart{last}"):
+        gath_start(last)
+    with scope(f"relayB{last}"):
+        relay(last, False)
     for s in range(nodes):
         with scope(f"finish{s}"):
             line_finish(s)
     with scope("drain"):
+        mask_copy.wait()
         for s in range(nodes):
             drain_blocks(s)
             line_drain(s)
@@ -516,15 +541,13 @@
             gath_all(s).wait_send()
 
 
-def put_out(structure_ref, y_ref, whole_ref, scale_ref, d_ref, off_ref, out_ref, off_buf, out_buf, sem):
+def put_out(mask_ref, y_ref, whole_ref, scale_ref, d_ref, off_ref, out_ref, off_buf, out_buf, sem):
     nodes, n_rows, seg, _ = whole_ref.shape
-    rows_local = off_ref.shape[1]
     copies = []
     for s in range(nodes):
-        row = find_row(structure_ref, s, lax.axis_index("prow"), n_rows, n_rows)
-        value = y_ref[s]
-        for r in range(rows_local):
-            off_buf[s, r] = jnp.where(row == r, value, jnp.zeros_like(value))
+        value = y_ref[s].astype(jnp.float32)
+        for r in range(off_ref.shape[1]):
+            off_buf[s, r] = jnp.where(mask_ref[s, r] > 0, value, 0.0).astype(jnp.bfloat16)
         copies.append(pltpu.make_async_copy(off_buf.at[s], off_ref.at[s], sem.at[0, s]))
         copies[-1].start()
         for k in range(n_rows):
@@ -553,18 +576,19 @@
     sends = ratio + n_cols // 2 - 1 + ratio
     operands = [pltpu.with_memory_space_constraint(x, pltpu.HBM) for x in (structure, inverse, panel)]
     anywhere = pl.BlockSpec(memory_space=pl.ANY)
-    smem = pl.BlockSpec(memory_space=pltpu.SMEM)
-    pieces, whole, scale = pl.pallas_call(
+    pieces, whole, scale, mask = pl.pallas_call(
         functools.partial(selected, n_rows, n_cols),
         out_shape=(
             jax.ShapeDtypeStruct((nodes, piece, width), bf16),
             jax.ShapeDtypeStruct((nodes, n_rows, seg, width), i16),
             jax.ShapeDtypeStruct((nodes, n_rows, 1, width), f32),
+            jax.ShapeDtypeStruct((nodes, rows_local, 1, width), f32),
         ),
         in_specs=[hbm] * 3,
-        out_specs=(anywhere, anywhere, anywhere),
+        out_specs=(anywhere,) * 4,
         scratch_shapes=[
             pltpu.SMEM(structure.shape, jnp.int32),
+            pltpu.VMEM((nodes, rows_local, 1, width), f32),
             pltpu.VMEM((nodes, piece, width), bf16),
             pltpu.VMEM((nodes, seg, width), i16),
             pltpu.VMEM((nodes, 1, width), f32),
@@ -588,7 +612,7 @@
             pltpu.VMEM((nodes, 1, width), f32),
             pltpu.VMEM((nodes, n_cols, seg, width), i16),
             pltpu.VMEM((nodes, n_cols, 1, width), f32),
-            dma, dma((nodes,)), dma((AHEAD,)), dma((nodes, 3)),
+            dma, dma, dma((nodes,)), dma((AHEAD,)), dma((nodes, 3)),
             dma((nodes, sends)), dma((nodes, ratio, SUB + 1)),
             dma((2, nodes)), dma((2, nodes)), dma((2, nodes, n_cols + 1)),
             *(dma((2, nodes)) for _ in range(6)),
@@ -604,7 +628,7 @@
             jax.ShapeDtypeStruct((nodes, rows_local, piece, width), bf16),
             jax.ShapeDtypeStruct(diag_inverse.shape, f32),
         ),
-        in_specs=[smem, vmem, vmem, vmem, vmem],
+        in_specs=[vmem] * 5,
         out_specs=(hbm, hbm),
         scratch_shapes=[
             pltpu.VMEM((nodes, rows_local, piece, width), bf16),
@@ -613,7 +637,7 @@
         ],
         compiler_params=pltpu.CompilerParams(vmem_limit_bytes=4 * 1024 * 1024),
         name="put_out",
-    )(structure, pieces, whole, scale, diag_inverse)
+    )(mask, pieces, whole, scale, diag_inverse)
 
 
 def solution(mesh):

time: 35.7 us -> 35.2 us (0.986)
  Pallas kernels: 34.8 us -> 34.4 us
    pallas_call x1, Pallas kernels: 1.62 us -> 1.03 us  [on_device(): pl.pallas_call(put_out, out_shape=(jax.ShapeDtypeStruct((nodes, rows_loca...]
where the time goes in v3:
time: 35.2 us; the launch traced here: 35 us
  Pallas kernels  34.4 us (98%)
  between operations  0.65 us (2%)
    pallas_call x1, Pallas kernels, on_device(): pl.pallas_call(functools.partial(selected, n_rows, n_cols), out_shape=(ja...  33.3 us
    pallas_call x1, Pallas kernels, on_device(): pl.pallas_call(put_out, out_shape=(jax.ShapeDtypeStruct((nodes, rows_loca...  1.03 us

profile of v3, /device:TPU:0, one launch (start us, length us, event | category | flops | bytes accessed | tf_op | source)
XLA Modules:
  0.0 35.0 jit_solution(95416961136941593)
XLA Ops:
  0.6 0.0 copy-start
  0.6 33.3 %selected_inverse.1 = (bf16[2,128,256]{2,1,0:T(8,128)(2,1)S(1)}, s16[2,8,32,256]{3,2,1,0:T(8,128)(2,1)S(1)}, f32[2,8,1,256]{3,2,1,0:T(1,128)S(1)}, f32[2,4,1,256]{3,2,1,0:T(1,128)S(1)}) custom-call(s32[2,8]{1,0:T(2,128)} %structure_hbm.1, bf16[4,512,8,512]{3,2,1,0:T(8,128)(2,1)} %inverse_ref.1, bf16[2,4,512,256]{3,2,1,0:T(8,128)(2,1)} %panel_ref.1), custom_call_target="tpu_custom_call" | custom-call | tf_op jit(solution)/shard_map/selected_inverse/pallas_call | solution.py:579
  34.0 0.0 copy-done
  34.0 1.0 %put_out.1 = (bf16[2,4,128,256]{3,2,1,0:T(8,128)(2,1)}, f32[2,256,256]{2,1,0:T(8,128)}) custom-call(f32[2,4,1,256]{3,2,1,0:T(1,128)S(1)} %get-tuple-element.6.mask_ref, bf16[2,128,256]{2,1,0:T(8,128)(2,1)S(1)} %get-tuple-element.7.y_ref, s16[2,8,32,256]{3,2,1,0:T(8,128)(2,1)S(1)} %get-tuple-element.8.whole_ref, ...), custom_call_target="tpu_custom_call" | custom-call | tf_op jit(solution)/shard_map/put_out/pallas_call | solution.py:625
Async XLA Ops:
  0.6 33.3 %copy-start = (f32[2,256,256]{2,1,0:T(8,128)S(1)}, f32[2,256,256]{2,1,0:T(8,128)}, u32[]{:S(2)}) copy-start(f32[2,256,256]{2,1,0:T(8,128)} %d_ref.1) | copy-start | bytes 1572868

commit v4 on v3

--- a/solution.py
+++ b/solution.py
@@ -8,7 +8,7 @@
 from jax.sharding import PartitionSpec as P
 
 MESH = pl.DeviceIdType.MESH
-SUB = 4
+SUB = 8
 STRIPS = 8
 AHEAD = 4
 FULL = 32700.0
@@ -472,7 +472,7 @@
     first = [(own_from_x, 0, u) for u in range(SUB)] + flow(0)
     chosen = 0
     for i, (step, s, u) in enumerate(first):
-        ready = STRIPS if i + 1 == len(first) else min(STRIPS, 2 + i)
+        ready = STRIPS if i + 1 == len(first) else min(STRIPS, 2 + i * 4 // SUB)
         with scope(f"choose{i}"):
             for k in range(chosen, ready):
                 choose(k)

time: 35.2 us -> 35 us (level)
  no operation moved by 1% of the time
where the time goes in v4:
time: 35 us; the launch traced here: 34.9 us
  Pallas kernels  34.2 us (98%)
  between operations  0.65 us (2%)
    pallas_call x1, Pallas kernels, on_device(): pl.pallas_call(functools.partial(selected, n_rows, n_cols), out_shape=(ja...  33.2 us
    pallas_call x1, Pallas kernels, on_device(): pl.pallas_call(put_out, out_shape=(jax.ShapeDtypeStruct((nodes, rows_loca...  1.03 us

profile of v4, /device:TPU:0, one launch (start us, length us, event | category | flops | bytes accessed | tf_op | source)
XLA Modules:
  0.0 34.9 jit_solution(13057639256882553423)
XLA Ops:
  0.6 0.0 copy-start
  0.6 33.2 %selected_inverse.1 = (bf16[2,128,256]{2,1,0:T(8,128)(2,1)S(1)}, s16[2,8,32,256]{3,2,1,0:T(8,128)(2,1)S(1)}, f32[2,8,1,256]{3,2,1,0:T(1,128)S(1)}, f32[2,4,1,256]{3,2,1,0:T(1,128)S(1)}) custom-call(s32[2,8]{1,0:T(2,128)} %structure_hbm.1, bf16[4,512,8,512]{3,2,1,0:T(8,128)(2,1)} %inverse_ref.1, bf16[2,4,512,256]{3,2,1,0:T(8,128)(2,1)} %panel_ref.1), custom_call_target="tpu_custom_call" | custom-call | tf_op jit(solution)/shard_map/selected_inverse/pallas_call | solution.py:579
  33.8 0.0 copy-done
  33.8 1.0 %put_out.1 = (bf16[2,4,128,256]{3,2,1,0:T(8,128)(2,1)}, f32[2,256,256]{2,1,0:T(8,128)}) custom-call(f32[2,4,1,256]{3,2,1,0:T(1,128)S(1)} %get-tuple-element.6.mask_ref, bf16[2,128,256]{2,1,0:T(8,128)(2,1)S(1)} %get-tuple-element.7.y_ref, s16[2,8,32,256]{3,2,1,0:T(8,128)(2,1)S(1)} %get-tuple-element.8.whole_ref, ...), custom_call_target="tpu_custom_call" | custom-call | tf_op jit(solution)/shard_map/put_out/pallas_call | solution.py:625
Async XLA Ops:
  0.6 33.2 %copy-start = (f32[2,256,256]{2,1,0:T(8,128)S(1)}, f32[2,256,256]{2,1,0:T(8,128)}, u32[]{:S(2)}) copy-start(f32[2,256,256]{2,1,0:T(8,128)} %d_ref.1) | copy-start | bytes 1572868

commit v5 on v4

--- a/solution.py
+++ b/solution.py
@@ -517,10 +517,10 @@
     for s in range(last):
         with scope(f"gathstart{s}"):
             gath_start(s)
+    with scope(f"gathstart{last}"):
+        gath_start(last)
     with scope(f"relayU{last}"):
         relay_early(last, False, slice(1, None))
-    with scope(f"gathstart{last}"):
-        gath_start(last)
     with scope(f"relayB{last}"):
         relay(last, False)
     for s in range(nodes):

time: 35 us -> 34.9 us (level)
  no operation moved by 1% of the time
where the time goes in v5:
time: 34.9 us; the launch traced here: 34.8 us
  Pallas kernels  34.1 us (98%)
  between operations  0.65 us (2%)
    pallas_call x1, Pallas kernels, on_device(): pl.pallas_call(functools.partial(selected, n_rows, n_cols), out_shape=(ja...  33.1 us
    pallas_call x1, Pallas kernels, on_device(): pl.pallas_call(put_out, out_shape=(jax.ShapeDtypeStruct((nodes, rows_loca...  1.03 us

profile of v5, /device:TPU:0, one launch (start us, length us, event | category | flops | bytes accessed | tf_op | source)
XLA Modules:
  0.0 34.8 jit_solution(13389399491575217121)
XLA Ops:
  0.6 0.0 copy-start
  0.6 33.1 %selected_inverse.1 = (bf16[2,128,256]{2,1,0:T(8,128)(2,1)S(1)}, s16[2,8,32,256]{3,2,1,0:T(8,128)(2,1)S(1)}, f32[2,8,1,256]{3,2,1,0:T(1,128)S(1)}, f32[2,4,1,256]{3,2,1,0:T(1,128)S(1)}) custom-call(s32[2,8]{1,0:T(2,128)} %structure_hbm.1, bf16[4,512,8,512]{3,2,1,0:T(8,128)(2,1)} %inverse_ref.1, bf16[2,4,512,256]{3,2,1,0:T(8,128)(2,1)} %panel_ref.1), custom_call_target="tpu_custom_call" | custom-call | tf_op jit(solution)/shard_map/selected_inverse/pallas_call | solution.py:579
  33.7 0.0 copy-done
  33.7 1.0 %put_out.1 = (bf16[2,4,128,256]{3,2,1,0:T(8,128)(2,1)}, f32[2,256,256]{2,1,0:T(8,128)}) custom-call(f32[2,4,1,256]{3,2,1,0:T(1,128)S(1)} %get-tuple-element.6.mask_ref, bf16[2,128,256]{2,1,0:T(8,128)(2,1)S(1)} %get-tuple-element.7.y_ref, s16[2,8,32,256]{3,2,1,0:T(8,128)(2,1)S(1)} %get-tuple-element.8.whole_ref, ...), custom_call_target="tpu_custom_call" | custom-call | tf_op jit(solution)/shard_map/put_out/pallas_call | solution.py:625
Async XLA Ops:
  0.6 33.1 %copy-start = (f32[2,256,256]{2,1,0:T(8,128)S(1)}, f32[2,256,256]{2,1,0:T(8,128)}, u32[]{:S(2)}) copy-start(f32[2,256,256]{2,1,0:T(8,128)} %d_ref.1) | copy-start | bytes 1572868
